TPU v7x, 256 devices: a whole 4x4x8 slice. The times are simulated.
256 devices in a mesh: batch: 32 (over z, x), tensor: 8 (over y, core).
Axes of the slice: x: 4, y: 4, z: 8, core: 2. Of those that a mesh axis runs over, the one named last changes fastest.
Arguments:
- tokens: bfloat16 [8192, 4096], P(('batch', 'tensor')), may hold values from -6 to 6
- norm_gain: float32 [4096], replicated, may hold values from 0.1 to 1.9
- w_query: bfloat16 [4096, 4096], P(None, 'tensor'), may hold values from -0.09375 to 0.09375
- w_key: bfloat16 [4096, 1024], P(None, 'tensor'), may hold values from -0.25 to 0.25
- w_value: bfloat16 [4096, 1024], P(None, 'tensor'), may hold values from -0.09375 to 0.09375
- w_out: bfloat16 [4096, 4096], P('tensor'), may hold values from -0.25 to 0.25
- prefix_keys: bfloat16 [16384, 1024], P('batch', 'tensor'), may hold values from -6 to 6
- prefix_values: bfloat16 [16384, 1024], P('batch', 'tensor'), may hold values from -6 to 6
- cache_keys: bfloat16 [147456, 1024], P('batch', 'tensor'), may hold values from -160 to 160
- cache_values: bfloat16 [147456, 1024], P('batch', 'tensor'), may hold values from -6 to 6
- cache_lengths: int32 [128], replicated, may hold values from 128 to 2048, as said below
- prefix_used: int32 [128], P('batch'), may hold values from 4096 to 16384
- parents: int32 [128, 64], P('batch'), may hold values from 0 to 62, as said below
- accepted_index: int32 [128, 8], P('batch'), may hold values from 0 to 63, as said below
Outputs:
- mixed_output: bfloat16 [8192, 4096], P(('batch', 'tensor'))
- accepted_keys: bfloat16 [128, 8, 1024], P('batch', None, 'tensor')
- accepted_values: bfloat16 [128, 8, 1024], P('batch', None, 'tensor')
Inputs may be any that keep to these rules, and one draw needn't show every extreme that they name: `cache_lengths`: within each aligned group of 4 requests at most 2 have more than 256 cached tokens; in the first group exactly that many do, and some request has exactly 2048. parents[r, 0] = 0; for i >= 1, parents[r, i] lies between max(0, i - 8) and i - 1. `accepted_index`: each row lists 8 tree positions, each the parent of the next, ending at a position of 32 or more; where the root is reached the row repeats 0 at its front.
All inputs are finite; a program needn't handle non-finite values.
Results may differ from a plain program's by a relative error of at most 0.015.
The roundings to bfloat16 on the way count: a program that leaves them out, or rounds other values in their place, can miss the bound.
Values may be sent and summed in bfloat16 or wider, within the bound.
A program may use at most 192 MiB of HBM per device.

v0:
```python
import jax
import jax.numpy as jnp
from jax import lax
from jax.sharding import PartitionSpec as P

HD = 128
NEG_FILL = -1e30
HIGHEST = lax.Precision.HIGHEST


def rms_normed(tokens, norm_gain):
    values = tokens.astype(jnp.float32)
    factor = lax.rsqrt(jnp.mean(values * values, axis=-1, keepdims=True) + 1e-05)
    return (values * factor * norm_gain).astype(jnp.bfloat16)


def ancestor_table(parents):
    node_count = parents.shape[-1]
    column = jnp.arange(node_count, dtype=jnp.int32)
    linked = (parents[..., None] == column).astype(jnp.float32)
    itself = (column[:, None] == column[None, :]).astype(jnp.float32)
    ancestry = jnp.minimum(linked + itself, 1.0)
    for repeat in range(node_count.bit_length()):
        ancestry = jnp.minimum(
            jnp.einsum("rij,rjk->rik", ancestry, ancestry, precision=HIGHEST), 1.0
        )
    return ancestry


def rotate(values, positions):
    half_width = values.shape[-1] // 2
    frequency = 10000.0 ** (-jnp.arange(half_width, dtype=jnp.float32) / half_width)
    angles = positions.astype(jnp.float32)[:, None] * frequency[None, :]
    cosine = jnp.cos(angles)[:, None, :]
    sine_table = jnp.sin(angles)[:, None, :]
    first_half = values[..., :half_width]
    second_half = values[..., half_width:]
    return jnp.concatenate(
        [
            first_half * cosine - second_half * sine_table,
            second_half * cosine + first_half * sine_table,
        ],
        axis=-1,
    )


def absorb(carry, scores, visible, apply_values):
    running_max, running_sum, running_out = carry
    masked = jnp.where(visible, scores, NEG_FILL)
    new_max = jnp.maximum(running_max, jnp.max(masked, axis=-1))
    weights = jnp.where(visible, jnp.exp(masked - new_max[..., None]), 0.0)
    factor = jnp.exp(running_max - new_max)
    new_sum = running_sum * factor + jnp.sum(weights, axis=-1)
    new_out = running_out * factor[..., None] + apply_values(weights.astype(jnp.bfloat16))
    return (new_max, new_sum, new_out)


def combine(first_part, second_part):
    joint_max = jnp.maximum(first_part[0], second_part[0])
    first_factor = jnp.exp(first_part[0] - joint_max)
    second_factor = jnp.exp(second_part[0] - joint_max)
    joint_sum = first_part[1] * first_factor + second_part[1] * second_factor
    joint_out = first_part[2] * first_factor[..., None] + second_part[2] * second_factor[..., None]
    return (joint_max, joint_sum, joint_out)


def empty_partials(leading, head_size):
    return (
        jnp.full(leading, NEG_FILL, jnp.float32),
        jnp.zeros(leading, jnp.float32),
        jnp.zeros(leading + (head_size,), jnp.float32),
    )


def cache_partials(queries, all_keys, all_values, lower_slot, upper_slot, score_scale):
    capacity = all_keys.shape[0]
    block_size = min(512, capacity)
    kv_local = queries.shape[1]
    head_size = queries.shape[3]

    def one_request(request_items):
        request_query, lower_bound, upper_bound = request_items
        blocks = (upper_bound - lower_bound + block_size - 1) // block_size

        def block_step(block_index, carry):
            block_begin = lower_bound + block_index * block_size
            start = jnp.clip(block_begin, 0, capacity - block_size)
            block_keys = lax.dynamic_slice_in_dim(all_keys, start, block_size, 0).reshape(
                block_size, kv_local, head_size
            )
            block_values = lax.dynamic_slice_in_dim(all_values, start, block_size, 0).reshape(
                block_size, kv_local, head_size
            )
            slot_ids = start + jnp.arange(block_size, dtype=jnp.int32)
            visible = (slot_ids >= block_begin) & (
                slot_ids < jnp.minimum(upper_bound, block_begin + block_size)
            )
            scores = (
                jnp.einsum(
                    "hqd,khd->hqk", request_query, block_keys, preferred_element_type=jnp.float32
                )
                * score_scale
            )
            return absorb(
                carry,
                scores,
                visible[None, None, :],
                lambda rounded: jnp.einsum(
                    "hqk,khd->hqd", rounded, block_values, preferred_element_type=jnp.float32
                ),
            )

        start_carry = empty_partials(request_query.shape[:2], head_size)
        return lax.fori_loop(0, blocks, block_step, start_carry)

    return lax.map(one_request, (queries, lower_slot, upper_slot))


def body(
    tokens,
    norm_gain,
    w_query,
    w_key,
    w_value,
    w_out,
    prefix_keys,
    prefix_values,
    cache_keys,
    cache_values,
    cache_lengths,
    prefix_used,
    parents,
    accepted_index,
):
    req_count, tree_size = parents.shape
    head_size = HD
    query_cols = w_query.shape[1]
    key_cols = w_key.shape[1]
    kv_local = key_cols // head_size
    group_size = query_cols // key_cols
    query_rows = tree_size * group_size
    score_scale = head_size ** (-0.5)
    normed = rms_normed(tokens, norm_gain)
    piece = lax.all_gather(normed, "tensor", axis=0, tiled=True)
    projected = jnp.concatenate(
        [
            jnp.dot(piece, w_query, preferred_element_type=jnp.float32),
            jnp.dot(piece, w_key, preferred_element_type=jnp.float32),
            jnp.dot(piece, w_value, preferred_element_type=jnp.float32),
        ],
        axis=1,
    )
    group_index = lax.axis_index("batch")
    own_lengths = lax.dynamic_slice_in_dim(cache_lengths, group_index * req_count, req_count)
    ancestry = ancestor_table(parents)
    tree_depth = (jnp.sum(ancestry, axis=-1) - 1.0).astype(jnp.int32)
    position = ((prefix_used + own_lengths)[:, None] + tree_depth).reshape(req_count * tree_size)
    queries = rotate(
        projected[:, :query_cols].reshape(-1, kv_local * group_size, head_size), position
    ).astype(jnp.bfloat16)
    queries = queries.reshape(req_count, tree_size, kv_local, group_size, head_size).transpose(
        0, 2, 1, 3, 4
    )
    queries = queries.reshape(req_count, kv_local, query_rows, head_size)
    new_keys = rotate(
        projected[:, query_cols : query_cols + key_cols].reshape(-1, kv_local, head_size), position
    ).astype(jnp.bfloat16)
    new_keys = new_keys.reshape(req_count, tree_size, key_cols)
    new_values = (
        projected[:, query_cols + key_cols :]
        .astype(jnp.bfloat16)
        .reshape(req_count, tree_size, key_cols)
    )
    accepted_keys = jnp.take_along_axis(new_keys, accepted_index[:, :, None], axis=1)
    accepted_values = jnp.take_along_axis(new_values, accepted_index[:, :, None], axis=1)
    tree_keys = new_keys.reshape(req_count, tree_size, kv_local, head_size)
    tree_values = new_values.reshape(req_count, tree_size, kv_local, head_size)
    tree_scores = (
        jnp.einsum("rhqd,rkhd->rhqk", queries, tree_keys, preferred_element_type=jnp.float32)
        * score_scale
    )
    tree_visible = jnp.repeat(ancestry > 0.5, group_size, axis=1)[:, None]
    tree_part = absorb(
        empty_partials((req_count, kv_local, query_rows), head_size),
        tree_scores,
        tree_visible,
        lambda rounded: jnp.einsum(
            "rhqk,rkhd->rhqd", rounded, tree_values, preferred_element_type=jnp.float32
        ),
    )
    own_offsets = jnp.cumsum(own_lengths) - own_lengths
    cache_part = cache_partials(
        queries, cache_keys, cache_values, own_offsets, own_offsets + own_lengths, score_scale
    )
    local_part = combine(tree_part, cache_part)
    piece_keys = lax.all_gather(prefix_keys, "batch", axis=0, tiled=True)
    piece_values = lax.all_gather(prefix_values, "batch", axis=0, tiled=True)
    row_count = piece_keys.shape[0]
    shaped_keys = piece_keys.reshape(row_count, kv_local, head_size)
    shaped_values = piece_values.reshape(row_count, kv_local, head_size)
    slot_ids = jnp.arange(row_count, dtype=jnp.int32)
    visible = (slot_ids[None, :] < prefix_used[:, None])[:, None, None, :]
    scores = (
        jnp.einsum("rhqd,khd->rhqk", queries, shaped_keys, preferred_element_type=jnp.float32)
        * score_scale
    )
    folded = absorb(
        local_part,
        scores,
        visible,
        lambda rounded: jnp.einsum(
            "rhqk,khd->rhqd", rounded, shaped_values, preferred_element_type=jnp.float32
        ),
    )
    attended = (folded[2] / folded[1][..., None]).astype(jnp.bfloat16)
    attended = attended.reshape(req_count, kv_local, tree_size, group_size, head_size).transpose(
        0, 2, 1, 3, 4
    )
    attended = attended.reshape(req_count * tree_size, query_cols)
    mixed_rows = lax.psum_scatter(
        jnp.dot(attended, w_out, preferred_element_type=jnp.float32).astype(jnp.bfloat16),
        "tensor",
        scatter_dimension=0,
        tiled=True,
    )
    return (mixed_rows, accepted_keys, accepted_values)


def solution(mesh):
    in_specs = (
        P(("batch", "tensor"), None),
        P(),
        P(None, "tensor"),
        P(None, "tensor"),
        P(None, "tensor"),
        P("tensor", None),
        P("batch", "tensor"),
        P("batch", "tensor"),
        P("batch", "tensor"),
        P("batch", "tensor"),
        P(),
        P("batch"),
        P("batch", None),
        P("batch", None),
    )
    out_specs = (
        P(("batch", "tensor"), None),
        P("batch", None, "tensor"),
        P("batch", None, "tensor"),
    )
    return jax.shard_map(body, mesh=mesh, in_specs=in_specs, out_specs=out_specs, check_vma=False)
```

profile of v0, /device:TPU:4, one launch (start us, length us, event | category | flops | bytes accessed | tf_op | source)
XLA Modules:
  0.0 278.1 jit_solution(979624814477540230)
XLA Ops:
  7.2 1.2 fusion.52
  8.4 1.8 fusion.54
  10.3 0.7 all-gather.6.cloned.1.call-update
  11.8 0.8 iota_compare_fusion
  12.6 0.8 dynamic-slice_add_fusion
  13.6 0.7 bitcast_subtract_fusion
  14.3 1.0 convolution_minimum_fusion.6
  18.2 23.1 %all-gather.4.cloned.1.call-done = bf16[256,4096]{1,0:T(8,128)(2,1)} async-done(((bf16[32,4096]{1,0:T(8,128)(2,1)}), bf16[256,4096]{1,0:T(8,128)(2,1)}) %all-gather.4.cloned.1.call-update) | async-done | bytes 2097168 | tf_op jit(solution)/shard_map/all_gather | solution.py:144
  41.3 4.1 %fusion.85 = f32[256,512]{1,0:T(8,128)S(1)} fusion(bf16[256,4096]{1,0:T(8,128)(2,1)} %all-gather.4.cloned.1.call-done, bf16[4096,512]{1,0:T(8,128)(2,1)} %param.22), kind=kOutput, calls=%fused_computation.133 | convolution fusion | flops 1073741824 | bytes 6815744 | tf_op jit(solution)/shard_map/dot_general | solution.py:147
  46.0 0.9 pad_maximum_fusion.1
  46.9 44.6 %while.69 = (s32[]{:T(128)}, f32[4,1,256]{2,1,0:T(1,128)S(1)}, f32[4,1,256]{2,1,0:T(1,128)S(1)}, f32[4,1,256,128]{3,2,1,0:T(8,128)}, s32[4]{0:T(128)S(1)}, /*ind...) while((s32[]{:T(128)}, f32[4,1,256]{2,1,0:T(1,128)S(1)}, ...), condition=%wide.region_9.10_spmd, body=%wide.region_4.9_spmd.sunk | while | flops 68356632 | bytes 2712316 | solution.py:116
  49.6 0.9 dynamic-slice_bitcast_fusion.3
  50.5 4.0 %while.70 = (s32[]{:T(128)}, f32[1,256]{1,0:T(1,128)S(1)}, f32[1,256]{1,0:T(1,128)S(1)}, f32[1,256,128]{2,1,0:T(8,128)S(1)}, s32[]{:T(128)}, /*index=5*/s32[]{:T...) while((s32[]{:T(128)}, f32[1,256]{1,0:T(1,128)S(1)}, ...), condition=%wide.region_8.8_spmd, body=%wide.region_5.7_spmd.sunk | while | flops 68356616 | bytes 2181353 | solution.py:114
  51.8 1.2 fusion.117
  53.2 1.3 fusion.119
  57.7 0.9 dynamic-slice_bitcast_fusion.3
  58.6 16.0 %while.70 = (s32[]{:T(128)}, f32[1,256]{1,0:T(1,128)S(1)}, f32[1,256]{1,0:T(1,128)S(1)}, f32[1,256,128]{2,1,0:T(8,128)S(1)}, s32[]{:T(128)}, /*index=5*/s32[]{:T...) while((s32[]{:T(128)}, f32[1,256]{1,0:T(1,128)S(1)}, ...), condition=%wide.region_8.8_spmd, body=%wide.region_5.7_spmd.sunk | while | flops 68356616 | bytes 2181353 | solution.py:114
  59.9 1.2 fusion.117
  61.2 1.3 fusion.119
  63.9 1.2 fusion.117
  65.2 1.3 fusion.119
  67.9 1.2 fusion.117
  69.2 1.3 fusion.119
  71.9 1.2 fusion.117
  73.2 1.3 fusion.119
  77.8 0.9 dynamic-slice_bitcast_fusion.3
  78.7 4.0 %while.70 = (s32[]{:T(128)}, f32[1,256]{1,0:T(1,128)S(1)}, f32[1,256]{1,0:T(1,128)S(1)}, f32[1,256,128]{2,1,0:T(8,128)S(1)}, s32[]{:T(128)}, /*index=5*/s32[]{:T...) while((s32[]{:T(128)}, f32[1,256]{1,0:T(1,128)S(1)}, ...), condition=%wide.region_8.8_spmd, body=%wide.region_5.7_spmd.sunk | while | flops 68356616 | bytes 2181353 | solution.py:114
  80.0 1.2 fusion.117
  81.3 1.3 fusion.119
  85.9 0.9 dynamic-slice_bitcast_fusion.3
  86.8 4.0 %while.70 = (s32[]{:T(128)}, f32[1,256]{1,0:T(1,128)S(1)}, f32[1,256]{1,0:T(1,128)S(1)}, f32[1,256,128]{2,1,0:T(8,128)S(1)}, s32[]{:T(128)}, /*index=5*/s32[]{:T...) while((s32[]{:T(128)}, f32[1,256]{1,0:T(1,128)S(1)}, ...), condition=%wide.region_8.8_spmd, body=%wide.region_5.7_spmd.sunk | while | flops 68356616 | bytes 2181353 | solution.py:114
  88.1 1.2 fusion.117
  89.4 1.3 fusion.119
  91.5 0.8 convolution_bitcast_fusion.1
  92.3 0.9 fusion.68
  93.3 1.5 copy.30
  94.8 1.5 copy.29
  96.3 1.0 pad_maximum_fusion.2
  97.8 1.3 fusion.84
  100.0 2.6 convolution_convert_fusion.1
  102.5 22.0 %all-gather.6.cloned.1.call-done = bf16[16384,128]{1,0:T(8,128)(2,1)} async-done(((bf16[512,128]{1,0:T(8,128)(2,1)}), bf16[16384,128]{1,0:T(8,128)(2,1)}) %all-gather.6.cloned.1.call-update) | async-done | bytes 4194320 | tf_op jit(solution)/shard_map/all_gather | solution.py:196
  124.5 27.2 %fusion.17 = (f32[4,256]{1,0:T(4,128)S(1)}, f32[4,256,16384]{2,1,0:T(8,128)}) fusion(pred[4,16384]{1,0:T(4,128)(4,1)S(1)} %iota_compare_fusion, bf16[16384,128]{1,0:T(8,128)(2,1)} %all-gather.6.cloned.1.call-done, bf16[4,256,64]{2,1,0:T(8,128)(2,1)} %bitcast.194, bf16[4,256,64]{2,1,0:T(8,128)(2,1)S(1)} %bitcast.191), kind=kOutput, calls=%fused_computation.30 | convolution fusion | flops 4345822208 | bytes 71634944 | tf_op jit(solution)/shard_map/rhqd,khd->rhqk/dot_general | solution.py:204
  151.8 24.3 %fusion.18 = f32[4,256]{1,0:T(4,128)S(1)} fusion(f32[4,256,16384]{2,1,0:T(8,128)} %get-tuple-element.336, f32[4,256]{1,0:T(4,128)S(1)} %get-tuple-element.337, pred[4,16384]{1,0:T(4,128)(4,1)S(1)} %iota_compare_fusion), kind=kLoop, calls=%fused_computation.31 | loop fusion | flops 83885056 | bytes 67182592 | tf_op jit(solution)/shard_map/reduce_sum | solution.py:53
  176.2 1.0 fusion.45
  177.3 28.4 %all-gather.8.cloned.1.call-done = bf16[16384,128]{1,0:T(8,128)(2,1)} async-done(((bf16[512,128]{1,0:T(8,128)(2,1)}), bf16[16384,128]{1,0:T(8,128)(2,1)}) %all-gather.8.cloned.1.call-update) | async-done | bytes 4194320 | tf_op jit(solution)/shard_map/all_gather | solution.py:197
  205.7 25.9 %fusion.46 = bf16[4,1,256,128]{3,2,0,1:T(8,128)(2,1)S(1)} fusion(f32[4,1,256,128]{3,2,0,1:T(8,128)S(1)} %fusion.45, bf16[16384,128]{1,0:T(8,128)(2,1)} %all-gather.8.cloned.1.call-done, f32[4,256,16384]{2,1,0:T(8,128)} %get-tuple-element.336, f32[4,256]{1,0:T(4,128)S(1)} %get-tuple-element.337, pred[4,16384]{1,0:T(4,128)(4,1)S(1)} %iota_compare_fusion, ...), kind=kOutput, calls=%fused_computation.48 | convolution fusion | flops 4379246592 | bytes 72163328 | tf_op jit(solution)/shard_map/rhqk,khd->rhqd/dot_general | solution.py:211
  231.8 4.8 %convolution_convert_fusion = bf16[256,4096]{1,0:T(8,128)(2,1)} fusion(bf16[256,512]{1,0:T(8,128)(2,1)S(1)} %reshape_transpose_reshape.4, bf16[512,4096]{1,0:T(8,128)(2,1)} %param.25), kind=kOutput, calls=%fused_computation.36 | convolution fusion | flops 1074790400 | bytes 6553600 | tf_op jit(solution)/shard_map/dot_general | solution.py:221
  238.8 32.8 %reduce-scatter.2.cloned.1.call-done = bf16[32,4096]{1,0:T(8,128)(2,1)} async-done(((bf16[256,4096]{1,0:T(8,128)(2,1)}), bf16[32,4096]{1,0:T(8,128)(2,1)}) %reduce-scatter.2.cloned.1.call-update) | async-done | bytes 262160 | tf_op jit(solution)/shard_map/reduce_scatter | solution.py:220
  (135 shorter events, 17.4 us)
Async XLA Ops:
  7.2 84.3 %copy-start = (bf16[4096,128]{1,0:T(8,128)(2,1)S(1)}, bf16[4096,128]{1,0:T(8,128)(2,1)}, u32[]{:S(2)}) copy-start(bf16[4096,128]{1,0:T(8,128)(2,1)} %param.23) | copy-start | bytes 3145732
  7.2 34.1 %all-gather.4.cloned.1.call-start = ((), (), s32[]{:S(2)}) async-start(), calls=%async_computation.1 | async-start | bytes 2359296 | tf_op jit(solution)/shard_map/all_gather | solution.py:144
  10.2 114.3 %all-gather.6.cloned.1.call-start = ((), (), s32[]{:S(2)}) async-start(), calls=%async_computation.2 | async-start | bytes 4325376 | tf_op jit(solution)/shard_map/all_gather | solution.py:196
  11.0 194.7 %all-gather.8.cloned.1.call-start = ((), (), s32[]{:S(2)}) async-start(), calls=%async_computation.3 | async-start | bytes 4325376 | tf_op jit(solution)/shard_map/all_gather | solution.py:197
  11.7 259.8 %reduce-scatter.2.cloned.1.call-start = ((), (), s32[]{:S(2)}) async-start(), calls=%async_computation.4 | async-start | bytes 2359296 | tf_op jit(solution)/shard_map/reduce_scatter | solution.py:220
  46.0 0.9 copy-start.2
  46.0 0.9 copy-start.4
  46.9 44.6 %copy-start.1 = (bf16[256,4096]{1,0:T(8,128)(2,1)S(1)}, bf16[256,4096]{1,0:T(8,128)(2,1)}, u32[]{:S(2)}) copy-start(bf16[256,4096]{1,0:T(8,128)(2,1)} %all-gather.4.cloned.1.call-done) | copy-start | bytes 6291460
  91.5 7.7 %copy-start.11 = (f32[4,1,256]{2,1,0:T(1,128)}, f32[4,1,256]{2,1,0:T(1,128)S(1)}, u32[]{:S(2)}) copy-start(f32[4,1,256]{2,1,0:T(1,128)S(1)} %get-tuple-element.269) | copy-start | bytes 12292
  91.5 33.1 %copy-start.3 = (bf16[256,4,64]{2,1,0:T(4,128)(2,1)S(1)}, bf16[256,4,64]{2,1,0:T(4,128)(2,1)}, u32[]{:S(2)}) copy-start(bf16[256,4,64]{2,1,0:T(4,128)(2,1)} %copy-done.2) | copy-start | bytes 393220
  97.2 0.6 copy-start.7
  99.2 0.7 copy-start.5
  151.8 24.4 %copy-start.12 = (f32[4,1,256]{2,1,0:T(1,128)S(1)}, f32[4,1,256]{2,1,0:T(1,128)}, u32[]{:S(2)}) copy-start(f32[4,1,256]{2,1,0:T(1,128)} %copy-done.11) | copy-start | bytes 12292
  151.8 24.5 %copy-start.6 = (f32[4,256,64]{1,2,0:T(8,128)S(1)}, f32[4,256,64]{1,2,0:T(8,128)}, u32[]{:S(2)}) copy-start(f32[4,256,64]{1,2,0:T(8,128)} %copy-done.5) | copy-start | bytes 786436
  151.8 24.4 %copy-start.9 = (bf16[256,128]{1,0:T(8,128)(2,1)S(1)}, bf16[256,128]{1,0:T(8,128)(2,1)}, u32[]{:S(2)}) copy-start(bf16[256,128]{1,0:T(8,128)(2,1)} %convolution_convert_fusion.1) | copy-start | bytes 196612
  151.8 24.4 %copy-start.10 = (f32[4,1,256,128]{3,2,1,0:T(8,128)S(1)}, f32[4,1,256,128]{3,2,1,0:T(8,128)}, u32[]{:S(2)}) copy-start(f32[4,1,256,128]{3,2,1,0:T(8,128)} %get-tuple-element.268) | copy-start | bytes 1572868
  231.8 4.9 %copy-start.13 = (s32[4,8]{1,0:T(4,128)S(1)}, s32[4,8]{1,0:T(4,128)}, u32[]{:S(2)}) copy-start(s32[4,8]{1,0:T(4,128)} %param.33) | copy-start | bytes 388
  231.8 5.6 %copy-start.8 = (bf16[4,64,128]{2,1,0:T(8,128)(2,1)S(1)}, bf16[4,64,128]{2,1,0:T(8,128)(2,1)}, u32[]{:S(2)}) copy-start(bf16[4,64,128]{2,1,0:T(8,128)(2,1)} %copy-done.7) | copy-start | bytes 196612
Sparse Core Ops, SparseCore 0:
  10.4 30.7 all-gather.3
  43.8 80.6 all-gather.5
  127.1 78.5 all-gather.7
  236.7 34.7 reduce-scatter.1
where the time goes:
time: 279 us; the launch traced here: 278 us
  waiting for transfers between devices  108 us (39%)
  matrix products  87.9 us (32%)
  other arithmetic  35.8 us (13%)
  local copies, waits for them, and re-layouts  17.8 us (6%)
  loops' own time  14.5 us (5%)
  between operations  14.2 us (5%)
    reduce_scatter x1, waiting for transfers between devices, body(): lax.psum_scatter(jnp.dot(attended, w_out, preferred_element_type=jnp.floa...  32.8 us
    all_gather x1, waiting for transfers between devices, body(): piece_values = lax.all_gather(prefix_values, 'batch', axis=0, tiled=True)  28.4 us
    dot_general x1, matrix products, body(): jnp.einsum('rhqd,khd->rhqk', queries, shaped_keys, preferred_element_type...  27.2 us
    dot_general x1, matrix products, body(): jnp.einsum('rhqk,khd->rhqd', rounded, shaped_values, preferred_element_ty...  25.9 us
    reduce_sum x9, other arithmetic, absorb(): new_sum = running_sum * factor + jnp.sum(weights, axis=-1)  25.5 us
    all_gather x1, waiting for transfers between devices, body(): piece = lax.all_gather(normed, 'tensor', axis=0, tiled=True)  23.1 us
    all_gather x1, waiting for transfers between devices, body(): piece_keys = lax.all_gather(prefix_keys, 'batch', axis=0, tiled=True)  22 us
    dot_general x7, matrix products, block_step(): jnp.einsum('hqk,khd->hqd', rounded, block_values, preferred_element_type=...  9.34 us
  transfers between devices with their start and end apart: 4, of which 4 were waited for; matrix products, arithmetic and copies ran while one was open for 38% of the time, Pallas kernels for 0%

commit v1 on v0

--- a/solution.py
+++ b/solution.py
@@ -6,6 +6,22 @@
 HD = 128
 NEG_FILL = -1e30
 HIGHEST = lax.Precision.HIGHEST
+
+
+def gather_around(x, axis, dim):
+    ways, here, step = (lax.axis_size(axis), lax.axis_index(axis), x.shape[dim])
+    lengths = [n * ways if d == dim else n for d, n in enumerate(x.shape)]
+    full = lax.dynamic_update_slice_in_dim(jnp.zeros(lengths, x.dtype), x, here * step, axis=dim)
+    going_up = going_down = x
+    for far in range(1, ways // 2 + 1):
+        going_up = lax.ppermute(going_up, axis, [(d, (d + 1) % ways) for d in range(ways)])
+        full = lax.dynamic_update_slice_in_dim(full, going_up, (here - far) % ways * step, axis=dim)
+        if 2 * far < ways:
+            going_down = lax.ppermute(going_down, axis, [(d, (d - 1) % ways) for d in range(ways)])
+            full = lax.dynamic_update_slice_in_dim(
+                full, going_down, (here + far) % ways * step, axis=dim
+            )
+    return full
 
 
 def rms_normed(tokens, norm_gain):
@@ -141,7 +157,7 @@
     query_rows = tree_size * group_size
     score_scale = head_size ** (-0.5)
     normed = rms_normed(tokens, norm_gain)
-    piece = lax.all_gather(normed, "tensor", axis=0, tiled=True)
+    piece = gather_around(normed, "tensor", 0)
     projected = jnp.concatenate(
         [
             jnp.dot(piece, w_query, preferred_element_type=jnp.float32),

time: 279 us -> 252 us (0.903)
  waiting for transfers between devices: 108 us -> 61.3 us
  starting transfers between devices: 0.16 us -> 8.99 us
  local copies, waits for them, and re-layouts: 17.8 us -> 26.5 us
    all_gather x1 -> x0, waiting for transfers between devices: 23.1 us -> none  [body(): piece = lax.all_gather(normed, 'tensor', axis=0, tiled=True)]
    all_gather x1, waiting for transfers between devices: 22 us -> 0.02 us  [body(): piece_keys = lax.all_gather(prefix_keys, 'batch', axis=0, tiled=True)]
    all_gather x1, waiting for transfers between devices: 28.4 us -> 11.3 us  [body(): piece_values = lax.all_gather(prefix_values, 'batch', axis=0, tiled=True)]
    ppermute x0 -> x7, waiting for transfers between devices: none -> 13.2 us  [the longest x4 13.2 us: gather_around(): lax.ppermute(going_up, axis, [(d, (d + 1) % ways) for d in range(ways)])]
    ppermute x0 -> x7, starting transfers between devices: none -> 8.87 us  [the longest x3 8.86 us: gather_around(): lax.ppermute(going_down, axis, [(d, (d - 1) % ways) for d in range(ways)])]
    dynamic_slice x8, local copies, waits for them, and re-layouts: 4.93 us -> 10.1 us  [cache_partials(): return lax.map(one_request, (queries, lower_slot, upper_slot))]
    reduce_scatter x1, waiting for transfers between devices: 32.8 us -> 36 us  [body(): lax.psum_scatter(jnp.dot(attended, w_out, preferred_element_type=jnp.floa...]
  transfers between devices with their start and end apart: 4 -> 10, of which waited for: 4 -> 5; matrix products, arithmetic and copies ran while one was open for 38% -> 48% of each run, Pallas kernels for 0% -> 0%
where the time goes in v1:
time: 252 us; the launch traced here: 251 us
  matrix products  87.1 us (35%)
  waiting for transfers between devices  61.3 us (24%)
  other arithmetic  38.2 us (15%)
  local copies, waits for them, and re-layouts  26.5 us (11%)
  loops' own time  14.3 us (6%)
  between operations  14.3 us (6%)
  starting transfers between devices  8.99 us (4%)
    reduce_scatter x1, waiting for transfers between devices, body(): lax.psum_scatter(jnp.dot(attended, w_out, preferred_element_type=jnp.floa...  36 us
    dot_general x1, matrix products, body(): jnp.einsum('rhqd,khd->rhqk', queries, shaped_keys, preferred_element_type...  27.1 us
    reduce_sum x9, other arithmetic, absorb(): new_sum = running_sum * factor + jnp.sum(weights, axis=-1)  26.4 us
    dot_general x1, matrix products, body(): jnp.einsum('rhqk,khd->rhqd', rounded, shaped_values, preferred_element_ty...  25.9 us
    ppermute x4, waiting for transfers between devices, gather_around(): lax.ppermute(going_up, axis, [(d, (d + 1) % ways) for d in range(ways)])  13.2 us
    all_gather x1, waiting for transfers between devices, body(): piece_values = lax.all_gather(prefix_values, 'batch', axis=0, tiled=True)  11.3 us
    dynamic_slice x8, local copies, waits for them, and re-layouts, cache_partials(): return lax.map(one_request, (queries, lower_slot, upper_slot))  10.1 us
    dot_general x7, matrix products, block_step(): jnp.einsum('hqk,khd->hqd', rounded, block_values, preferred_element_type=...  9.36 us
  transfers between devices with their start and end apart: 10, of which 5 were waited for; matrix products, arithmetic and copies ran while one was open for 48% of the time, Pallas kernels for 0%

profile of v1, /device:TPU:4, one launch (start us, length us, event | category | flops | bytes accessed | tf_op | source)
XLA Modules:
  0.0 250.6 jit_solution(16129968212883265237)
XLA Ops:
  8.0 1.1 fusion.52
  9.4 1.8 constant_dynamic-update-slice_fusion.7
  11.2 3.0 %collective-permute-start.1 = (bf16[32,4096]{1,0:T(8,128)(2,1)}, bf16[32,4096]{1,0:T(8,128)(2,1)}, u32[]{:S(2)}, u32[]{:S(2)}) collective-permute-start(bf16[32,4096]{1,0:T(8,128)(2,1)} %get-tuple-element.313), channel_id=1, source_target_pairs={{0,7},{1,0},{2,1},{3,2},{4,3},{5,4},{6,5},{7,6},{8,15},{9,8},{10,9... | collective-permute-start | bytes 786440 | tf_op jit(solution)/shard_map/ppermute | solution.py:20
  14.2 1.0 convolution_minimum_fusion.6
  17.9 1.3 bitcast_subtract_fusion
  20.0 1.2 multiply_cosine_fusion
  21.2 3.0 %collective-permute-start.3 = (bf16[32,4096]{1,0:T(8,128)(2,1)}, bf16[32,4096]{1,0:T(8,128)(2,1)S(1)}, u32[]{:S(2)}, u32[]{:S(2)}) collective-permute-start(bf16[32,4096]{1,0:T(8,128)(2,1)} %collective-permute-done.1), channel_id=1, source_target_pairs={{0,7},{1,0},{2,1},{3,2},{4,3},{5,4},{6,5},{7,6},{8,15},{9,8},{10,9... | collective-permute-start | bytes 786440 | tf_op jit(solution)/shard_map/ppermute | solution.py:20
  26.1 2.3 collective-permute-done.2
  28.4 3.0 %collective-permute-start.5 = (bf16[32,4096]{1,0:T(8,128)(2,1)S(1)}, bf16[32,4096]{1,0:T(8,128)(2,1)S(1)}, u32[]{:S(2)}, u32[]{:S(2)}) collective-permute-start(bf16[32,4096]{1,0:T(8,128)(2,1)S(1)} %collective-permute-done.3), channel_id=1, source_target_pairs={{0,7},{1,0},{2,1},{3,2},{4,3},{5,4},{6,5},{7,6},{8,15},{9,8},{10,9... | collective-permute-start | bytes 786440 | tf_op jit(solution)/shard_map/ppermute | solution.py:20
  31.4 4.0 %collective-permute-done.4 = bf16[32,4096]{1,0:T(8,128)(2,1)S(1)} collective-permute-done((bf16[32,4096]{1,0:T(8,128)(2,1)S(1)}, bf16[32,4096]{1,0:T(8,128)(2,1)S(1)}, u32[]{:S(2)}, u32[]{:S(2)}) %collective-permute-start.4) | collective-permute-done | bytes 262176 | tf_op jit(solution)/shard_map/ppermute | solution.py:17
  35.4 6.9 %collective-permute-done.6 = bf16[32,4096]{1,0:T(8,128)(2,1)S(1)} collective-permute-done((bf16[32,4096]{1,0:T(8,128)(2,1)S(1)}, bf16[32,4096]{1,0:T(8,128)(2,1)S(1)}, u32[]{:S(2)}, u32[]{:S(2)}) %collective-permute-start.6) | collective-permute-done | bytes 262176 | tf_op jit(solution)/shard_map/ppermute | solution.py:17
  44.4 4.2 %fusion.86 = f32[256,512]{1,0:T(8,128)} fusion(bf16[256,4096]{1,0:T(8,128)(2,1)S(1)} %constant_dynamic-update-slice_fusion, bf16[4096,512]{1,0:T(8,128)(2,1)} %param.22), kind=kOutput, calls=%fused_computation.141 | convolution fusion | flops 1073741824 | bytes 6815744 | tf_op jit(solution)/shard_map/dot_general | solution.py:163
  48.7 2.0 reshape.401
  51.6 1.7 subtract_convert_fusion
  56.4 51.8 %while.69 = (s32[]{:T(128)}, f32[4,1,256]{2,1,0:T(1,128)S(1)}, f32[4,1,256]{2,1,0:T(1,128)}, f32[4,1,256,128]{3,2,1,0:T(8,128)}, s32[4]{0:T(128)}, /*index=5*/s3...) while((s32[]{:T(128)}, f32[4,1,256]{2,1,0:T(1,128)S(1)}, ...), condition=%wide.region_9.10_spmd, body=%wide.region_4.0_spmd.sunk | while | flops 68356632 | bytes 2713316 | solution.py:132
  56.4 1.3 dynamic_slice.58
  57.7 1.3 dynamic_slice.59
  61.1 4.0 %while.70 = (s32[]{:T(128)}, f32[1,256]{1,0:T(1,128)S(1)}, f32[1,256]{1,0:T(1,128)S(1)}, f32[1,256,128]{2,1,0:T(8,128)S(1)}, s32[]{:T(128)}, /*index=5*/s32[]{:T...) while((s32[]{:T(128)}, f32[1,256]{1,0:T(1,128)S(1)}, ...), condition=%wide.region_8.8_spmd, body=%wide.region_5.7_spmd.sunk | while | flops 68356616 | bytes 2181345 | solution.py:130
  62.4 1.2 fusion.118
  63.8 1.3 fusion.120
  66.4 1.3 dynamic_slice.58
  67.6 1.3 dynamic_slice.59
  71.1 16.0 %while.70 = (s32[]{:T(128)}, f32[1,256]{1,0:T(1,128)S(1)}, f32[1,256]{1,0:T(1,128)S(1)}, f32[1,256,128]{2,1,0:T(8,128)S(1)}, s32[]{:T(128)}, /*index=5*/s32[]{:T...) while((s32[]{:T(128)}, f32[1,256]{1,0:T(1,128)S(1)}, ...), condition=%wide.region_8.8_spmd, body=%wide.region_5.7_spmd.sunk | while | flops 68356616 | bytes 2181345 | solution.py:130
  72.4 1.2 fusion.118
  73.7 1.3 fusion.120
  76.4 1.2 fusion.118
  77.7 1.3 fusion.120
  80.4 1.2 fusion.118
  81.7 1.3 fusion.120
  84.4 1.2 fusion.118
  85.7 1.3 fusion.120
  88.3 1.3 dynamic_slice.58
  89.6 1.3 dynamic_slice.59
  93.0 4.0 %while.70 = (s32[]{:T(128)}, f32[1,256]{1,0:T(1,128)S(1)}, f32[1,256]{1,0:T(1,128)S(1)}, f32[1,256,128]{2,1,0:T(8,128)S(1)}, s32[]{:T(128)}, /*index=5*/s32[]{:T...) while((s32[]{:T(128)}, f32[1,256]{1,0:T(1,128)S(1)}, ...), condition=%wide.region_8.8_spmd, body=%wide.region_5.7_spmd.sunk | while | flops 68356616 | bytes 2181345 | solution.py:130
  94.3 1.2 fusion.118
  95.7 1.3 fusion.120
  98.3 1.3 dynamic_slice.58
  99.6 1.3 dynamic_slice.59
  103.0 4.0 %while.70 = (s32[]{:T(128)}, f32[1,256]{1,0:T(1,128)S(1)}, f32[1,256]{1,0:T(1,128)S(1)}, f32[1,256,128]{2,1,0:T(8,128)S(1)}, s32[]{:T(128)}, /*index=5*/s32[]{:T...) while((s32[]{:T(128)}, f32[1,256]{1,0:T(1,128)S(1)}, ...), condition=%wide.region_8.8_spmd, body=%wide.region_5.7_spmd.sunk | while | flops 68356616 | bytes 2181345 | solution.py:130
  104.3 1.2 fusion.118
  105.6 1.3 fusion.120
  108.2 1.9 convolution_convert_fusion.1
  111.2 27.1 %fusion.17 = (f32[4,256]{1,0:T(4,128)S(1)}, f32[4,256,16384]{2,1,0:T(8,128)}) fusion(pred[4,16384]{1,0:T(4,128)(4,1)S(1)} %iota_compare_fusion, bf16[16384,128]{1,0:T(8,128)(2,1)} %all-gather.3.cloned.1.call-done, bf16[4,256,64]{2,1,0:T(8,128)(2,1)} %bitcast.194, bf16[4,256,64]{2,1,0:T(8,128)(2,1)} %bitcast.191), kind=kOutput, calls=%fused_computation.30 | convolution fusion | flops 4345822208 | bytes 71634944 | tf_op jit(solution)/shard_map/rhqd,khd->rhqk/dot_general | solution.py:220
  138.4 24.2 %fusion.18 = f32[4,256]{1,0:T(4,128)S(1)} fusion(f32[4,256,16384]{2,1,0:T(8,128)} %get-tuple-element.338, f32[4,256]{1,0:T(4,128)S(1)} %get-tuple-element.339, pred[4,16384]{1,0:T(4,128)(4,1)S(1)} %iota_compare_fusion), kind=kLoop, calls=%fused_computation.31 | loop fusion | flops 83885056 | bytes 67182592 | tf_op jit(solution)/shard_map/reduce_sum | solution.py:69
  163.8 11.3 %all-gather.5.cloned.1.call-done = bf16[16384,128]{1,0:T(8,128)(2,1)} async-done(((bf16[512,128]{1,0:T(8,128)(2,1)}), bf16[16384,128]{1,0:T(8,128)(2,1)}) %all-gather.5.cloned.1.call-update) | async-done | bytes 4194320 | tf_op jit(solution)/shard_map/all_gather | solution.py:213
  175.1 25.9 %fusion.46 = bf16[4,1,256,128]{3,2,0,1:T(8,128)(2,1)S(1)} fusion(f32[4,1,256,128]{3,2,0,1:T(8,128)S(1)} %fusion.45, bf16[16384,128]{1,0:T(8,128)(2,1)} %all-gather.5.cloned.1.call-done, f32[4,256,16384]{2,1,0:T(8,128)} %get-tuple-element.338, f32[4,256]{1,0:T(4,128)S(1)} %get-tuple-element.339, pred[4,16384]{1,0:T(4,128)(4,1)S(1)} %iota_compare_fusion, ...), kind=kOutput, calls=%fused_computation.48 | convolution fusion | flops 4379246592 | bytes 72163328 | tf_op jit(solution)/shard_map/rhqk,khd->rhqd/dot_general | solution.py:227
  201.1 4.8 %convolution_convert_fusion = bf16[256,4096]{1,0:T(8,128)(2,1)} fusion(bf16[256,512]{1,0:T(8,128)(2,1)S(1)} %reshape_transpose_reshape.4, bf16[512,4096]{1,0:T(8,128)(2,1)} %param.25), kind=kOutput, calls=%fused_computation.36 | convolution fusion | flops 1074790400 | bytes 6553600 | tf_op jit(solution)/shard_map/dot_general | solution.py:237
  208.1 36.0 %reduce-scatter.2.cloned.1.call-done = bf16[32,4096]{1,0:T(8,128)(2,1)} async-done(((bf16[256,4096]{1,0:T(8,128)(2,1)}), bf16[32,4096]{1,0:T(8,128)(2,1)}) %reduce-scatter.2.cloned.1.call-update) | async-done | bytes 262160 | tf_op jit(solution)/shard_map/reduce_scatter | solution.py:236
  (146 shorter events, 26.6 us)
Async XLA Ops:
  7.2 35.2 %copy-start = (bf16[4096,128]{1,0:T(8,128)(2,1)S(1)}, bf16[4096,128]{1,0:T(8,128)(2,1)}, u32[]{:S(2)}) copy-start(bf16[4096,128]{1,0:T(8,128)(2,1)} %param.23) | copy-start | bytes 3145732
  7.2 9.8 %copy-start.8 = (s32[4]{0:T(128)S(1)}, s32[4]{0:T(128)}, u32[]{:S(2)}) copy-start(s32[4]{0:T(128)} %param.31) | copy-start | bytes 52
  7.2 9.9 %copy-start.9 = (s32[128]{0:T(128)S(1)}, s32[128]{0:T(128)}, u32[]{:S(2)}) copy-start(s32[128]{0:T(128)} %param.30) | copy-start | bytes 1540
  7.2 104.0 %all-gather.3.cloned.1.call-start = ((), (), s32[]{:S(2)}) async-start(), calls=%async_computation.1 | async-start | bytes 4325376 | tf_op jit(solution)/shard_map/all_gather | solution.py:212
  7.9 167.1 %all-gather.5.cloned.1.call-start = ((), (), s32[]{:S(2)}) async-start(), calls=%async_computation.2 | async-start | bytes 4325376 | tf_op jit(solution)/shard_map/all_gather | solution.py:213
  11.2 10.0 %collective-permute-start = (bf16[32,4096]{1,0:T(8,128)(2,1)}, bf16[32,4096]{1,0:T(8,128)(2,1)}, u32[]{:S(2)}, u32[]{:S(2)}) collective-permute-start(bf16[32,4096]{1,0:T(8,128)(2,1)} %get-tuple-element.313), channel_id=1, source_target_pairs={{0,1},{1,2},{2,3},{3,4},{4,5},{5,6},{6,7},{7,0},{8,9},{9,10},{10,1... | collective-permute-start | bytes 786440 | tf_op jit(solution)/shard_map/ppermute | solution.py:17
  11.2 10.0 %collective-permute-start.1 = (bf16[32,4096]{1,0:T(8,128)(2,1)}, bf16[32,4096]{1,0:T(8,128)(2,1)}, u32[]{:S(2)}, u32[]{:S(2)}) collective-permute-start(bf16[32,4096]{1,0:T(8,128)(2,1)} %get-tuple-element.313), channel_id=1, source_target_pairs={{0,7},{1,0},{2,1},{3,2},{4,3},{5,4},{6,5},{7,6},{8,15},{9,8},{10,9... | collective-permute-start | bytes 786440 | tf_op jit(solution)/shard_map/ppermute | solution.py:20
  14.1 230.0 %reduce-scatter.2.cloned.1.call-start = ((), (), s32[]{:S(2)}) async-start(), calls=%async_computation.3 | async-start | bytes 2359296 | tf_op jit(solution)/shard_map/reduce_scatter | solution.py:236
  21.1 7.2 %collective-permute-start.2 = (bf16[32,4096]{1,0:T(8,128)(2,1)}, bf16[32,4096]{1,0:T(8,128)(2,1)S(1)}, u32[]{:S(2)}, u32[]{:S(2)}) collective-permute-start(bf16[32,4096]{1,0:T(8,128)(2,1)} %collective-permute-done), channel_id=1, source_target_pairs={{0,1},{1,2},{2,3},{3,4},{4,5},{5,6},{6,7},{7,0},{8,9},{9,10},{10,1... | collective-permute-start | bytes 786440 | tf_op jit(solution)/shard_map/ppermute | solution.py:17
  21.2 7.2 %collective-permute-start.3 = (bf16[32,4096]{1,0:T(8,128)(2,1)}, bf16[32,4096]{1,0:T(8,128)(2,1)S(1)}, u32[]{:S(2)}, u32[]{:S(2)}) collective-permute-start(bf16[32,4096]{1,0:T(8,128)(2,1)} %collective-permute-done.1), channel_id=1, source_target_pairs={{0,7},{1,0},{2,1},{3,2},{4,3},{5,4},{6,5},{7,6},{8,15},{9,8},{10,9... | collective-permute-start | bytes 786440 | tf_op jit(solution)/shard_map/ppermute | solution.py:20
  28.4 7.0 %collective-permute-start.4 = (bf16[32,4096]{1,0:T(8,128)(2,1)S(1)}, bf16[32,4096]{1,0:T(8,128)(2,1)S(1)}, u32[]{:S(2)}, u32[]{:S(2)}) collective-permute-start(bf16[32,4096]{1,0:T(8,128)(2,1)S(1)} %collective-permute-done.2), channel_id=1, source_target_pairs={{0,1},{1,2},{2,3},{3,4},{4,5},{5,6},{6,7},{7,0},{8,9},{9,10},{10,1... | collective-permute-start | bytes 786440 | tf_op jit(solution)/shard_map/ppermute | solution.py:17
  28.4 7.0 %collective-permute-start.5 = (bf16[32,4096]{1,0:T(8,128)(2,1)S(1)}, bf16[32,4096]{1,0:T(8,128)(2,1)S(1)}, u32[]{:S(2)}, u32[]{:S(2)}) collective-permute-start(bf16[32,4096]{1,0:T(8,128)(2,1)S(1)} %collective-permute-done.3), channel_id=1, source_target_pairs={{0,7},{1,0},{2,1},{3,2},{4,3},{5,4},{6,5},{7,6},{8,15},{9,8},{10,9... | collective-permute-start | bytes 786440 | tf_op jit(solution)/shard_map/ppermute | solution.py:20
  35.4 7.0 %collective-permute-start.6 = (bf16[32,4096]{1,0:T(8,128)(2,1)S(1)}, bf16[32,4096]{1,0:T(8,128)(2,1)S(1)}, u32[]{:S(2)}, u32[]{:S(2)}) collective-permute-start(bf16[32,4096]{1,0:T(8,128)(2,1)S(1)} %collective-permute-done.4), channel_id=1, source_target_pairs={{0,1},{1,2},{2,3},{3,4},{4,5},{5,6},{6,7},{7,0},{8,9},{9,10},{10,1... | collective-permute-start | bytes 786440 | tf_op jit(solution)/shard_map/ppermute | solution.py:17
  53.3 1.6 copy-start.1
  53.3 2.5 copy-start.2
  138.4 24.3 %copy-start.6 = (f32[4,1,256]{2,1,0:T(1,128)S(1)}, f32[4,1,256]{2,1,0:T(1,128)}, u32[]{:S(2)}) copy-start(f32[4,1,256]{2,1,0:T(1,128)} %get-tuple-element.269) | copy-start | bytes 12292
  138.4 24.4 %copy-start.3 = (f32[4,256,64]{1,2,0:T(8,128)S(1)}, f32[4,256,64]{1,2,0:T(8,128)}, u32[]{:S(2)}) copy-start(f32[4,256,64]{1,2,0:T(8,128)} %get-tuple-element.336) | copy-start | bytes 786436
  138.4 24.4 %copy-start.4 = (f32[4,1,256,128]{3,2,1,0:T(8,128)S(1)}, f32[4,1,256,128]{3,2,1,0:T(8,128)}, u32[]{:S(2)}) copy-start(f32[4,1,256,128]{3,2,1,0:T(8,128)} %get-tuple-element.268) | copy-start | bytes 1572868
  138.4 24.4 %copy-start.5 = (f32[4,256]{1,0:T(4,128)S(1)}, f32[4,256]{1,0:T(4,128)}, u32[]{:S(2)}) copy-start(f32[4,256]{1,0:T(4,128)} %get-tuple-element.325) | copy-start | bytes 12292
  201.1 4.8 %copy-start.7 = (s32[4,8]{1,0:T(4,128)S(1)}, s32[4,8]{1,0:T(4,128)}, u32[]{:S(2)}) copy-start(s32[4,8]{1,0:T(4,128)} %param.33) | copy-start | bytes 388
Sparse Core Ops, SparseCore 0:
  10.6 83.1 all-gather.2
  96.4 78.6 all-gather.4
  206.1 38.0 reduce-scatter.1
